TPU v7x, 32 devices: a whole 2x2x4 slice. The times are simulated.
32 devices in a mesh: rep: 4 (over x, core), shard: 8 (over z, y).
Axes of the slice: x: 2, y: 2, z: 4, core: 2. Of those that a mesh axis runs over, the one named last changes fastest.
Arguments:
- tokens: bfloat16 [4096, 896], P(('rep', 'shard')), may hold values from -6 to 6
- cotangent: bfloat16 [4096, 896], P(('rep', 'shard')), may hold values from -6 to 6
- lengths: int32 [32, 8], P(('rep', 'shard')), may hold values from 1 to 64, 128 in all within a row
- query_weight: bfloat16 [896, 896], P('shard'), may hold values from -0.1875 to 0.1875
- key_weight: bfloat16 [896, 128], P('shard'), may hold values from -0.1875 to 0.1875
- value_weight: bfloat16 [896, 128], P('shard'), may hold values from -0.1875 to 0.1875
- output_weight: bfloat16 [896, 896], P('shard'), may hold values from -0.5 to 0.5
- query_bias: bfloat16 [896], P('shard'), may hold values from -3 to 3
- key_bias: bfloat16 [128], P('shard'), may hold values from -3 to 3
- value_bias: bfloat16 [128], P('shard'), may hold values from -3 to 3
- attn_gain: bfloat16 [896], P('shard'), may hold values from 0.5 to 1.5
- gate_weight: bfloat16 [896, 4864], P('shard'), may hold values from -0.1875 to 0.1875
- up_weight: bfloat16 [896, 4864], P('shard'), may hold values from -0.1875 to 0.1875
- down_weight: bfloat16 [4864, 896], P('shard'), may hold values from -0.15625 to 0.15625
- mlp_gain: bfloat16 [896], P('shard'), may hold values from 0.5 to 1.5
Outputs:
- result: bfloat16 [4096, 896], P(('rep', 'shard'))
- grad_tokens: float32 [4096, 896], P(('rep', 'shard'))
- grad_query_weight: float32 [896, 896], P('shard')
- grad_key_weight: float32 [896, 128], P('shard')
- grad_value_weight: float32 [896, 128], P('shard')
- grad_output_weight: float32 [896, 896], P('shard')
- grad_query_bias: float32 [896], P('shard')
- grad_key_bias: float32 [128], P('shard')
- grad_value_bias: float32 [128], P('shard')
- grad_attn_gain: float32 [896], P('shard')
- grad_gate_weight: float32 [896, 4864], P('shard')
- grad_up_weight: float32 [896, 4864], P('shard')
- grad_down_weight: float32 [4864, 896], P('shard')
- grad_mlp_gain: float32 [896], P('shard')
Inputs may be any that keep to these rules, and one draw needn't show every extreme that they name: Row b lists the lengths of the 8 sequences packed in order on the b-th block of 128 tokens; they fill it exactly, and the longest of every row is exactly 64.
All inputs are finite; a program needn't handle non-finite values.
Results may differ from a plain program's by a relative error of at most 0.02.
The roundings to bfloat16 on the way count: a program that leaves them out, or rounds other values in their place, can miss the bound.
Values may be sent and summed in bfloat16 or wider, within the bound.
A program may use at most 192 MiB of HBM per device.

v0:
```python
import math
import jax
import jax.numpy as jnp
from jax import lax
from jax.sharding import PartitionSpec as P

HEADS = 14
KVH = 2
HD = 64
theta_base = 1000000.0
eps_norm = 1e-06
masked_score = -1000000000.0


def times_transposed(left, weight):
    return lax.dot_general(
        left, weight, (((1,), (1,)), ((), ())), preferred_element_type=jnp.float32
    )


def tables(lengths_row, rows):
    ends = jnp.cumsum(lengths_row)
    starts = ends - lengths_row
    places = jnp.arange(rows, dtype=jnp.int32)
    inside = ((places[:, None] >= starts[None, :]) & (places[:, None] < ends[None, :])).astype(
        jnp.int32
    )
    slots = jnp.arange(lengths_row.shape[0], dtype=jnp.int32)
    segment = jnp.sum(inside * slots[None, :], axis=1)
    first = jnp.sum(inside * starts[None, :], axis=1)
    offset = (places - first).astype(jnp.float32)
    half = HD // 2
    freq = theta_base ** (-(jnp.arange(half, dtype=jnp.float32) * (2.0 / HD)))
    angles = offset[:, None] * freq[None, :]
    return (segment, places, jnp.cos(angles), jnp.sin(angles))


def rotate(values, cosine, sine):
    half = values.shape[-1] // 2
    first, second = (values[..., :half], values[..., half:])
    cosine = cosine[:, :, None, :]
    sine = sine[:, :, None, :]
    return jnp.concatenate(
        [first * cosine - second * sine, second * cosine + first * sine], axis=-1
    )


def unrotate(grads, cosine, sine):
    half = grads.shape[-1] // 2
    first, second = (grads[..., :half], grads[..., half:])
    cosine = cosine[:, :, None, :]
    sine = sine[:, :, None, :]
    return jnp.concatenate(
        [first * cosine + second * sine, second * cosine - first * sine], axis=-1
    )


def norm_fwd(hidden, gain):
    scale = lax.rsqrt(jnp.mean(hidden * hidden, axis=-1, keepdims=True) + eps_norm)
    return (scale, hidden * scale * gain.astype(jnp.float32))


def norm_bwd(dnormed, hidden, scale, gain):
    gain_f = gain.astype(jnp.float32)
    dgain = jnp.sum(dnormed * hidden * scale, axis=0)
    inner = dnormed * gain_f
    dhidden = scale * inner - hidden * (scale * scale * scale) * jnp.mean(
        inner * hidden, axis=-1, keepdims=True
    )
    return (dhidden, dgain)


def scores_of(query, keys, segment, places):
    raw = jnp.einsum("igha,jga->ghij", query, keys, preferred_element_type=jnp.float32) * (
        1.0 / math.sqrt(HD)
    )
    allowed = (segment[:, None] == segment[None, :]) & (places[None, :] <= places[:, None])
    return jnp.where(allowed[None, None], raw, masked_score)


def attend(query, keys, values, segment, places):
    raw = scores_of(query, keys, segment, places)
    top = jnp.max(raw, axis=-1, keepdims=True)
    total = jnp.sum(jnp.exp(raw - top), axis=-1)
    lse = top[..., 0] + jnp.log(total)
    probs = jnp.exp(raw - lse[..., None]).astype(jnp.bfloat16)
    mixed = jnp.einsum("ghij,jga->igha", probs, values, preferred_element_type=jnp.float32).astype(
        jnp.bfloat16
    )
    return (mixed, lse)


def attend_back(query, keys, values, mixed, dmixed, lse, segment, places):
    raw = scores_of(query, keys, segment, places)
    probs_f = jnp.exp(raw - lse[..., None])
    probs = probs_f.astype(jnp.bfloat16)
    dvals = jnp.einsum("ghij,igha->jga", probs, dmixed, preferred_element_type=jnp.float32)
    dprobs = jnp.einsum("igha,jga->ghij", dmixed, values, preferred_element_type=jnp.float32)
    delta = jnp.einsum("igha,igha->ghi", dmixed, mixed, preferred_element_type=jnp.float32)
    dscores = (probs_f * (dprobs - delta[..., None]) * (1.0 / math.sqrt(HD))).astype(jnp.bfloat16)
    dquery = jnp.einsum("ghij,jga->igha", dscores, keys, preferred_element_type=jnp.float32)
    dkeys = jnp.einsum("ghij,igha->jga", dscores, query, preferred_element_type=jnp.float32)
    return (dquery, dkeys, dvals)


def pad_rows(vector, rows):
    return jnp.pad(vector, (0, rows - vector.shape[0]))


def share_of(weight, index, shards, shares):
    width = weight.shape[1] // shards
    part = width // shares
    return jnp.concatenate(
        [
            lax.dynamic_slice(weight, (0, s * width + index * part), (weight.shape[0], part))
            for s in range(shards)
        ],
        axis=1,
    )


def on_device(
    tokens,
    cotangent,
    lengths,
    query_weight,
    key_weight,
    value_weight,
    output_weight,
    query_bias,
    key_bias,
    value_bias,
    attn_gain,
    gate_weight,
    up_weight,
    down_weight,
    mlp_gain,
):
    shards = lax.axis_size("shard")
    reps = lax.axis_size("rep")
    rep = lax.axis_index("rep")
    rows, width = tokens.shape
    own = query_weight.shape[0]
    kvd = key_weight.shape[1]
    own_kv = key_bias.shape[0]
    small_w = 128
    f32, bf16 = (jnp.float32, jnp.bfloat16)
    small = jnp.stack(
        [query_bias, attn_gain, mlp_gain, pad_rows(key_bias, own), pad_rows(value_bias, own)],
        axis=1,
    )
    small = jnp.pad(small, ((0, 0), (0, small_w - small.shape[1])))
    packed = jnp.concatenate([query_weight, key_weight, value_weight, output_weight, small], axis=1)
    packed = lax.all_gather(packed, "shard", axis=0, tiled=True)
    wide = width + 2 * kvd
    qkv_weight = packed[:, :wide]
    output_full = packed[:, wide : wide + width]
    vectors = packed[:, wide + width : wide + width + 5].T
    query_bias_f, attn_gain_f, mlp_gain_f = (vectors[0], vectors[1], vectors[2])
    key_bias_f = vectors[3].reshape(shards, own)[:, :own_kv].reshape(kvd)
    value_bias_f = vectors[4].reshape(shards, own)[:, :own_kv].reshape(kvd)
    qkv_bias = jnp.concatenate([query_bias_f, key_bias_f, value_bias_f]).astype(f32)
    part = down_weight.shape[0] // reps
    gate_mine = lax.all_gather(
        share_of(gate_weight, rep, shards, reps), "shard", axis=0, tiled=True
    )
    up_mine = lax.all_gather(share_of(up_weight, rep, shards, reps), "shard", axis=0, tiled=True)
    down_mine = lax.all_gather(
        lax.dynamic_slice(down_weight, (rep * part, 0), (part, width)), "shard", axis=0, tiled=True
    )
    cot_all = lax.all_gather(cotangent, "rep", axis=0, tiled=True)
    segment, places, cosine, sine = jax.vmap(lambda lens: tables(lens, rows))(lengths)
    flat = tokens.astype(f32)
    scale_one, normed_one = norm_fwd(flat, attn_gain_f)
    normed_one = normed_one.astype(bf16)
    qkv = jnp.dot(normed_one, qkv_weight, preferred_element_type=f32) + qkv_bias
    query = rotate(qkv[:, :width].reshape(1, rows, HEADS, HD), cosine, sine).astype(bf16)
    query = query.reshape(1, rows, KVH, HEADS // KVH, HD)
    keys = rotate(qkv[:, width : width + kvd].reshape(1, rows, KVH, HD), cosine, sine).astype(bf16)
    values = qkv[:, width + kvd :].reshape(1, rows, KVH, HD).astype(bf16)
    mixed, lse = jax.vmap(attend)(query, keys, values, segment, places)
    mixed_flat = mixed.reshape(rows, width)
    hidden_one = flat + jnp.dot(mixed_flat, output_full, preferred_element_type=f32)
    scale_two, normed_two = norm_fwd(hidden_one, mlp_gain_f)
    normed_all = lax.all_gather(normed_two.astype(bf16), "rep", axis=0, tiled=True)
    gate = jnp.dot(normed_all, gate_mine, preferred_element_type=f32)
    upper = jnp.dot(normed_all, up_mine, preferred_element_type=f32)
    sigma = jax.nn.sigmoid(gate)
    product = (gate * sigma * upper).astype(bf16)
    dprod = times_transposed(cot_all, down_mine)
    dgate = (dprod * upper * sigma * (1.0 + gate * (1.0 - sigma))).astype(bf16)
    dup = (dprod * gate * sigma).astype(bf16)
    dnormed_part = times_transposed(dgate, gate_mine) + times_transposed(dup, up_mine)
    dnormed_two = lax.psum_scatter(
        dnormed_part.astype(bf16), "rep", scatter_dimension=0, tiled=True
    ).astype(f32)
    grad_down = jnp.dot(product.T, cot_all, preferred_element_type=f32).astype(bf16)
    grad_gate = jnp.dot(normed_all.T, dgate, preferred_element_type=f32).astype(bf16)
    grad_up = jnp.dot(normed_all.T, dup, preferred_element_type=f32).astype(bf16)
    down_owned = lax.psum_scatter(grad_down, "shard", scatter_dimension=0, tiled=True)
    gate_owned = lax.psum_scatter(grad_gate, "shard", scatter_dimension=0, tiled=True)
    up_owned = lax.psum_scatter(grad_up, "shard", scatter_dimension=0, tiled=True)
    out_part = jnp.dot(product, down_mine, preferred_element_type=f32).astype(bf16)
    out_sum = lax.psum_scatter(out_part, "rep", scatter_dimension=0, tiled=True)
    result = (hidden_one + out_sum.astype(f32)).astype(bf16)
    dh_two, grad_mlp_gain = norm_bwd(dnormed_two, hidden_one, scale_two, mlp_gain_f)
    dhidden = cotangent.astype(f32) + dh_two
    dres = dhidden.astype(bf16)
    grad_output = jnp.dot(mixed_flat.T, dres, preferred_element_type=f32).astype(bf16)
    dmixed = times_transposed(dres, output_full).astype(bf16)
    dmixed = dmixed.reshape(1, rows, KVH, HEADS // KVH, HD)
    dquery, dkeys, dvals = jax.vmap(attend_back)(
        query, keys, values, mixed, dmixed, lse, segment, places
    )
    dquery = unrotate(dquery.reshape(1, rows, HEADS, HD), cosine, sine).reshape(rows, width)
    dkeys = unrotate(dkeys, cosine, sine).reshape(rows, kvd)
    dvals = dvals.reshape(rows, kvd)
    dqkv = jnp.concatenate([dquery, dkeys, dvals], axis=1)
    grad_bias = jnp.sum(dqkv, axis=0)
    dqkv_b = dqkv.astype(bf16)
    grad_qkv = jnp.dot(normed_one.T, dqkv_b, preferred_element_type=f32).astype(bf16)
    dnormed_one = times_transposed(dqkv_b, qkv_weight)
    dh_one, grad_attn_gain = norm_bwd(dnormed_one, flat, scale_one, attn_gain_f)
    grad_input = dhidden + dh_one
    spread = lambda v: jnp.pad(v.reshape(shards, own_kv), ((0, 0), (0, own - own_kv))).reshape(
        width
    )
    small_g = jnp.stack(
        [
            grad_bias[:width],
            grad_attn_gain,
            grad_mlp_gain,
            spread(grad_bias[width : width + kvd]),
            spread(grad_bias[width + kvd :]),
        ],
        axis=0,
    )
    small_g = jnp.pad(small_g, ((0, small_w - small_g.shape[0]), (0, 0))).T.astype(bf16)
    packed_g = jnp.concatenate([grad_qkv, grad_output, small_g], axis=1)
    owned = lax.psum_scatter(packed_g, "shard", scatter_dimension=0, tiled=True)
    total_w = wide + width
    share_w = total_w // reps
    chunks = [
        jnp.concatenate([owned[:, i * share_w : (i + 1) * share_w], owned[:, total_w:]], axis=1)
        for i in range(reps)
    ]
    split = lax.psum_scatter(
        jnp.concatenate(chunks, axis=0), "rep", scatter_dimension=0, tiled=True
    )
    vec = split[:, share_w : share_w + 5].astype(f32).T
    attn_all = lax.all_gather(split[:, :share_w], "rep", axis=0)
    attn_all = jnp.concatenate([attn_all[i] for i in range(reps)], axis=1).astype(f32)
    down_all = lax.all_gather(down_owned, "rep", axis=0, tiled=True).astype(f32)

    def joined(share):
        every = lax.all_gather(share, "rep", axis=0)
        return jnp.concatenate(
            [every[r][:, s * part : (s + 1) * part] for s in range(shards) for r in range(reps)],
            axis=1,
        ).astype(f32)

    return (
        result,
        grad_input,
        attn_all[:, :width],
        attn_all[:, width : width + kvd],
        attn_all[:, width + kvd : wide],
        attn_all[:, wide:],
        vec[0],
        vec[3][:own_kv],
        vec[4][:own_kv],
        vec[1],
        joined(gate_owned),
        joined(up_owned),
        down_all,
        vec[2],
    )


def solution(mesh):
    in_specs = (
        P(("rep", "shard"), None),
        P(("rep", "shard"), None),
        P(("rep", "shard"), None),
        P("shard", None),
        P("shard", None),
        P("shard", None),
        P("shard", None),
        P("shard"),
        P("shard"),
        P("shard"),
        P("shard"),
        P("shard", None),
        P("shard", None),
        P("shard", None),
        P("shard"),
    )
    out_specs = (
        P(("rep", "shard"), None),
        P(("rep", "shard"), None),
        P("shard", None),
        P("shard", None),
        P("shard", None),
        P("shard", None),
        P("shard"),
        P("shard"),
        P("shard"),
        P("shard"),
        P("shard", None),
        P("shard", None),
        P("shard", None),
        P("shard"),
    )
    return jax.shard_map(
        on_device, mesh=mesh, in_specs=in_specs, out_specs=out_specs, check_vma=False
    )
```

profile of v0, /device:TPU:0, one launch (start us, length us, event | category | flops | bytes accessed | tf_op | source)
XLA Modules:
  0.0 711.2 jit_solution(1980135578788501737)
XLA Ops:
  8.8 0.9 constant_dynamic-update-slice_fusion.3
  11.3 1.0 constant_dynamic-update-slice_fusion
  13.2 1.9 constant_dynamic-slice_fusion.1
  15.1 0.9 concatenate.94
  16.1 0.9 concatenate.95
  18.5 11.2 %all_gather.44 = bf16[512,896]{1,0:T(8,128)(2,1)} all-gather(bf16[128,896]{1,0:T(8,128)(2,1)S(1)} %copy-done.7), channel_id=1, replica_groups=mesh['rep'=4,'shard'=8] {'rep'}, dimensions={0}, use_global_device_ids=true | all-gather | bytes 1146880 | tf_op jit(solution)/shard_map/all_gather | solution.py:171
  29.9 55.2 %all-gather.11.cloned.1.call-done = bf16[896,2176]{1,0:T(8,128)(2,1)} async-done(((bf16[112,2176]{1,0:T(8,128)(2,1)}), bf16[896,2176]{1,0:T(8,128)(2,1)}) %all-gather.11.cloned.1.call-update) | async-done | bytes 3899408 | tf_op jit(solution)/shard_map/all_gather | solution.py:154
  85.1 1.0 slice_bitcast_fusion
  87.2 2.1 convolution_add_fusion
  90.7 2.0 multiply_reduce_fusion
  92.8 9.9 %all_gather.40 = bf16[512,896]{1,0:T(8,128)(2,1)} all-gather(bf16[128,896]{1,0:T(8,128)(2,1)S(1)} %multiply_convert_fusion.3), channel_id=1, replica_groups=mesh['rep'=4,'shard'=8] {'rep'}, dimensions={0}, use_global_device_ids=true | all-gather | bytes 1146880 | tf_op jit(solution)/shard_map/all_gather | solution.py:185
  102.7 34.8 %all-gather.13.cloned.1.call-done = bf16[896,1216]{1,0:T(8,128)(2,1)} async-done(((bf16[112,1216]{1,0:T(8,128)(2,1)}), bf16[896,1216]{1,0:T(8,128)(2,1)}) %all-gather.13.cloned.1.call-update) | async-done | bytes 2179088 | tf_op jit(solution)/shard_map/all_gather | solution.py:164
  137.5 4.9 fusion.66
  142.4 47.5 %all-gather.15.cloned.1.call-done = bf16[896,1216]{1,0:T(8,128)(2,1)} async-done(((bf16[112,1216]{1,0:T(8,128)(2,1)}), bf16[896,1216]{1,0:T(8,128)(2,1)}) %all-gather.15.cloned.1.call-update) | async-done | bytes 2179088 | tf_op jit(solution)/shard_map/all_gather | solution.py:167
  189.8 5.0 fusion.67
  194.8 46.3 %all-gather.17.cloned.1.call-done = bf16[1216,896]{1,0:T(8,128)(2,1)} async-done(((bf16[152,896]{1,0:T(8,128)(2,1)}), bf16[1216,896]{1,0:T(8,128)(2,1)}) %all-gather.17.cloned.1.call-update) | async-done | bytes 2179088 | tf_op jit(solution)/shard_map/all_gather | solution.py:168
  241.1 7.0 multiply_convert_fusion
  248.1 1.6 fusion.68
  250.7 2.6 add_convert_fusion
  253.3 4.5 convolution_convert_fusion.5
  257.9 4.5 convolution_convert_fusion.1
  262.5 4.4 convolution_convert_fusion.2
  267.1 4.5 convolution_convert_fusion
  271.7 4.2 reduce-scatter.12.cloned.1.call-done
  275.9 1.1 fusion.27
  277.1 25.3 %reduce-scatter.10.cloned.1.call-done = bf16[128,896]{1,0:T(8,128)(2,1)} async-done(((bf16[512,896]{1,0:T(8,128)(2,1)}), bf16[128,896]{1,0:T(8,128)(2,1)}) %reduce-scatter.10.cloned.1.call-update) | async-done | bytes 229392 | tf_op jit(solution)/shard_map/reduce_scatter | solution.py:204
  302.4 1.9 fusion.24
  304.3 2.0 fusion.17
  308.0 1.4 copy-done.3
  312.7 2.1 pad_maximum_fusion
  314.8 60.8 %reduce-scatter.20.cloned.1.call-done = bf16[112,1216]{1,0:T(8,128)(2,1)} async-done(((bf16[896,1216]{1,0:T(8,128)(2,1)}), bf16[112,1216]{1,0:T(8,128)(2,1)}) %reduce-scatter.20.cloned.1.call-update) | async-done | bytes 272400 | tf_op jit(solution)/shard_map/reduce_scatter | solution.py:202
  375.7 72.2 %reduce-scatter.18.cloned.1.call-done = bf16[112,1216]{1,0:T(8,128)(2,1)} async-done(((bf16[896,1216]{1,0:T(8,128)(2,1)}), bf16[112,1216]{1,0:T(8,128)(2,1)}) %reduce-scatter.18.cloned.1.call-update) | async-done | bytes 272400 | tf_op jit(solution)/shard_map/reduce_scatter | solution.py:201
  448.0 77.8 %reduce-scatter.22.cloned.1.call-done = bf16[152,896]{1,0:T(8,128)(2,1)} async-done(((bf16[1216,896]{1,0:T(8,128)(2,1)}), bf16[152,896]{1,0:T(8,128)(2,1)}) %reduce-scatter.22.cloned.1.call-update) | async-done | bytes 272400
  525.8 86.8 %reduce-scatter.14.cloned.1.call-done = bf16[112,2176]{1,0:T(8,128)(2,1)} async-done(((bf16[896,2176]{1,0:T(8,128)(2,1)}), bf16[112,2176]{1,0:T(8,128)(2,1)}) %reduce-scatter.14.cloned.1.call-update) | async-done | bytes 487440 | tf_op jit(solution)/shard_map/reduce_scatter | solution.py:240
  614.3 1.0 fusion.62
  616.3 1.0 fusion.34
  617.2 14.0 %all-gather.23.cloned.1.call-done = bf16[448,1216]{1,0:T(8,128)(2,1)} async-done(((bf16[112,1216]{1,0:T(8,128)(2,1)}), bf16[448,1216]{1,0:T(8,128)(2,1)}) %all-gather.23.cloned.1.call-update) | async-done | bytes 1089552 | tf_op jit(solution)/shard_map/all_gather | solution.py:256
  631.2 1.6 fusion.59
  633.3 3.9 concatenate.107
  637.2 1.5 convert_element_type.175
  638.7 11.2 %all-gather.21.cloned.1.call-done = bf16[448,1216]{1,0:T(8,128)(2,1)} async-done(((bf16[112,1216]{1,0:T(8,128)(2,1)}), bf16[448,1216]{1,0:T(8,128)(2,1)}) %all-gather.21.cloned.1.call-update) | async-done | bytes 1089552 | tf_op jit(solution)/shard_map/all_gather | solution.py:256
  649.9 1.6 fusion.61
  652.0 3.8 concatenate.106
  655.9 1.5 convert_element_type.173
  657.4 11.1 %all-gather.19.cloned.1.call-done = bf16[608,896]{1,0:T(8,128)(2,1)} async-done(((bf16[152,896]{1,0:T(8,128)(2,1)}), bf16[608,896]{1,0:T(8,128)(2,1)}) %all-gather.19.cloned.1.call-update) | async-done | bytes 1089552 | tf_op jit(solution)/shard_map/all_gather | solution.py:253
  668.4 2.7 convert_element_type.177
  671.2 21.6 %reduce-scatter.16.cloned.1.call-done = bf16[112,640]{1,0:T(8,128)(2,1)} async-done(((bf16[448,640]{1,0:T(8,128)(2,1)}), bf16[112,640]{1,0:T(8,128)(2,1)}) %reduce-scatter.16.cloned.1.call-update) | async-done | bytes 143376 | tf_op jit(solution)/shard_map/reduce_scatter | solution.py:247
  695.9 6.5 all-gather
  (134 shorter events, 23.7 us)
Async XLA Ops:
  7.2 9.9 %copy-start = (bf16[608,896]{1,0:T(8,128)(2,1)S(1)}, bf16[608,896]{1,0:T(8,128)(2,1)}, u32[]{:S(2)}) copy-start(bf16[608,896]{1,0:T(8,128)(2,1)} %param.28) | copy-start | bytes 3268612
  7.2 77.9 %all-gather.11.cloned.1.call-start = ((), (), s32[]{:S(2)}) async-start(), calls=%async_computation.7 | async-start | bytes 4386816 | tf_op jit(solution)/shard_map/all_gather | solution.py:154
  12.3 0.8 copy-start.6
  13.1 124.4 %all-gather.13.cloned.1.call-start = ((), (), s32[]{:S(2)}) async-start(), calls=%async_computation.8 | async-start | bytes 2580480 | tf_op jit(solution)/shard_map/all_gather | solution.py:164
  13.2 4.8 copy-start.10
  13.2 5.1 copy-start.2
  13.2 5.3 copy-start.7
  16.0 173.8 %all-gather.15.cloned.1.call-start = ((), (), s32[]{:S(2)}) async-start(), calls=%async_computation.9 | async-start | bytes 2580480 | tf_op jit(solution)/shard_map/all_gather | solution.py:167
  17.1 224.0 %all-gather.17.cloned.1.call-start = ((), (), s32[]{:S(2)}) async-start(), calls=%async_computation.10 | async-start | bytes 2451456 | tf_op jit(solution)/shard_map/all_gather | solution.py:168
  17.9 258.0 %reduce-scatter.12.cloned.1.call-start = ((), (), s32[]{:S(2)}) async-start(), calls=%async_computation.12 | async-start | bytes 1146880 | tf_op jit(solution)/shard_map/reduce_scatter | solution.py:194
  241.1 7.0 copy-start.8
  248.1 1.6 copy-start.11
  248.1 1.6 copy-start.12
  248.1 2.5 copy-start.9
  253.3 49.1 %reduce-scatter.10.cloned.1.call-start = ((), (), s32[]{:S(2)}) async-start(), calls=%async_computation.11 | async-start | bytes 1146880 | tf_op jit(solution)/shard_map/reduce_scatter | solution.py:204
  257.8 117.8 %reduce-scatter.20.cloned.1.call-start = ((), (), s32[]{:S(2)}) async-start(), calls=%async_computation.16 | async-start | bytes 2580480 | tf_op jit(solution)/shard_map/reduce_scatter | solution.py:202
  262.4 185.5 %reduce-scatter.18.cloned.1.call-start = ((), (), s32[]{:S(2)}) async-start(), calls=%async_computation.15 | async-start | bytes 2580480 | tf_op jit(solution)/shard_map/reduce_scatter | solution.py:201
  266.9 258.9 %reduce-scatter.22.cloned.1.call-start = ((), (), s32[]{:S(2)}) async-start(), calls=%async_computation.20 | async-start | bytes 2451456
  271.6 341.0 %reduce-scatter.14.cloned.1.call-start = ((), (), s32[]{:S(2)}) async-start(), calls=%async_computation.13 | async-start | bytes 4386816 | tf_op jit(solution)/shard_map/reduce_scatter | solution.py:240
  307.3 2.1 copy-start.3
  314.7 316.5 %all-gather.23.cloned.1.call-start = ((), (), s32[]{:S(2)}) async-start(), calls=%async_computation.19 | async-start | bytes 1433600 | tf_op jit(solution)/shard_map/all_gather | solution.py:256
  375.6 274.3 %all-gather.21.cloned.1.call-start = ((), (), s32[]{:S(2)}) async-start(), calls=%async_computation.18 | async-start | bytes 1433600 | tf_op jit(solution)/shard_map/all_gather | solution.py:256
  447.9 220.5 %all-gather.19.cloned.1.call-start = ((), (), s32[]{:S(2)}) async-start(), calls=%async_computation.17 | async-start | bytes 1361920 | tf_op jit(solution)/shard_map/all_gather | solution.py:253
  525.8 167.0 %reduce-scatter.16.cloned.1.call-start = ((), (), s32[]{:S(2)}) async-start(), calls=%async_computation.14 | async-start | bytes 716800 | tf_op jit(solution)/shard_map/reduce_scatter | solution.py:247
  631.2 1.7 copy-start.5
  649.9 1.7 copy-start.4
  695.8 8.8 %copy-start.1 = (bf16[608,896]{1,0:T(8,128)(2,1)S(1)}, bf16[608,896]{1,0:T(8,128)(2,1)}, u32[]{:S(2)}) copy-start(bf16[608,896]{1,0:T(8,128)(2,1)} %param.28) | copy-start | bytes 3268612
Sparse Core Ops, SparseCore 0:
  13.2 71.7 all-gather.10
  87.8 49.6 all-gather.12
  140.3 49.5 all-gather.14
  192.5 48.5 all-gather.16
  253.4 22.4 reduce-scatter.11
  278.3 23.9 reduce-scatter.9
  305.9 69.6 reduce-scatter.19
  379.1 68.7 reduce-scatter.17
  451.9 73.7 reduce-scatter.21
  529.1 83.4 reduce-scatter.13
  614.2 16.9 all-gather.22
  632.6 17.2 all-gather.20
  651.5 16.9 all-gather.18
  670.8 21.9 reduce-scatter.15
where the time goes:
time: 712 us; the launch traced here: 711 us
  waiting for transfers between devices  569 us (80%)
  matrix products  49 us (7%)
  local copies, waits for them, and re-layouts  33.5 us (5%)
  blocking collectives  27.6 us (4%)
  other arithmetic  16.8 us (2%)
  between operations  14.4 us (2%)
    reduce_scatter x1, waiting for transfers between devices, on_device(): owned = lax.psum_scatter(packed_g, 'shard', scatter_dimension=0, tiled=True)  86.8 us
    unnamed x15, waiting for transfers between devices  78 us
    reduce_scatter x1, waiting for transfers between devices, on_device(): lax.psum_scatter(grad_gate, 'shard', scatter_dimension=0, tiled=True)  72.2 us
    reduce_scatter x1, waiting for transfers between devices, on_device(): lax.psum_scatter(grad_up, 'shard', scatter_dimension=0, tiled=True)  60.8 us
    all_gather x1, waiting for transfers between devices, on_device(): packed = lax.all_gather(packed, 'shard', axis=0, tiled=True)  55.2 us
    all_gather x1, waiting for transfers between devices, on_device(): lax.all_gather(share_of(up_weight, rep, shards, reps), 'shard', axis=0, t...  47.5 us
    all_gather x1, waiting for transfers between devices, on_device(): lax.all_gather(lax.dynamic_slice(down_weight, (rep * part, 0), (part, wid...  46.3 us
    all_gather x1, waiting for transfers between devices, on_device(): lax.all_gather(share_of(gate_weight, rep, shards, reps), 'shard', axis=0,...  34.8 us
  transfers between devices with their start and end apart: 14, of which 14 were waited for; matrix products, arithmetic and copies ran while one was open for 10% of the time, Pallas kernels for 0%

commit v1 on v0

--- a/solution.py
+++ b/solution.py
@@ -151,7 +151,14 @@
     )
     small = jnp.pad(small, ((0, 0), (0, small_w - small.shape[1])))
     packed = jnp.concatenate([query_weight, key_weight, value_weight, output_weight, small], axis=1)
-    packed = lax.all_gather(packed, "shard", axis=0, tiled=True)
+    ring = [packed]
+    for hop in range(7):
+        ring.append(lax.ppermute(ring[-1], "shard", [(dev, (dev + 1) % 8) for dev in range(8)]))
+    packed = jnp.roll(
+        jnp.concatenate(ring[::-1], axis=0),
+        (lax.axis_index("shard") + 1) * ring[0].shape[0],
+        axis=0,
+    )
     wide = width + 2 * kvd
     qkv_weight = packed[:, :wide]
     output_full = packed[:, wide : wide + width]

time: 712 us -> 682 us (0.958)
  waiting for transfers between devices: 569 us -> 533 us
    ppermute x0 -> x7, waiting for transfers between devices: none -> 119 us  [on_device(): lax.ppermute(ring[-1], 'shard', [(dev, (dev + 1) % 8) for dev in range(8)])]
    all_gather x1 -> x0, waiting for transfers between devices: 55.2 us -> none  [on_device(): packed = lax.all_gather(packed, 'shard', axis=0, tiled=True)]
    all_gather x1, waiting for transfers between devices: 47.5 us -> 0.01 us  [on_device(): lax.all_gather(share_of(up_weight, rep, shards, reps), 'shard', axis=0, t...]
    all_gather x1, waiting for transfers between devices: 34.8 us -> 0.01 us  [on_device(): lax.all_gather(share_of(gate_weight, rep, shards, reps), 'shard', axis=0,...]
    all_gather x1, waiting for transfers between devices: 46.3 us -> 31.2 us  [on_device(): lax.all_gather(lax.dynamic_slice(down_weight, (rep * part, 0), (part, wid...]
    unnamed x15 -> x14, waiting for transfers between devices: 78 us -> 78.2 us
  transfers between devices with their start and end apart: 14 -> 20, of which waited for: 14 -> 18; matrix products, arithmetic and copies ran while one was open for 10% -> 12% of each run, Pallas kernels for 0% -> 0%
where the time goes in v1:
time: 682 us; the launch traced here: 681 us
  waiting for transfers between devices  533 us (78%)
  matrix products  51.7 us (8%)
  local copies, waits for them, and re-layouts  33.2 us (5%)
  blocking collectives  25.4 us (4%)
  other arithmetic  19.1 us (3%)
  between operations  14.8 us (2%)
    ppermute x7, waiting for transfers between devices, on_device(): lax.ppermute(ring[-1], 'shard', [(dev, (dev + 1) % 8) for dev in range(8)])  119 us
    reduce_scatter x1, waiting for transfers between devices, on_device(): owned = lax.psum_scatter(packed_g, 'shard', scatter_dimension=0, tiled=True)  87.1 us
    unnamed x14, waiting for transfers between devices  78.2 us
    reduce_scatter x1, waiting for transfers between devices, on_device(): lax.psum_scatter(grad_gate, 'shard', scatter_dimension=0, tiled=True)  72.2 us
    reduce_scatter x1, waiting for transfers between devices, on_device(): lax.psum_scatter(grad_up, 'shard', scatter_dimension=0, tiled=True)  60.2 us
    all_gather x1, waiting for transfers between devices, on_device(): lax.all_gather(lax.dynamic_slice(down_weight, (rep * part, 0), (part, wid...  31.2 us
    reduce_scatter x1, waiting for transfers between devices, on_device(): out_sum = lax.psum_scatter(out_part, 'rep', scatter_dimension=0, tiled=True)  25.3 us
    all_gather x2, waiting for transfers between devices, joined(): every = lax.all_gather(share, 'rep', axis=0)  23.8 us
  transfers between devices with their start and end apart: 20, of which 18 were waited for; matrix products, arithmetic and copies ran while one was open for 12% of the time, Pallas kernels for 0%

profile of v1, /device:TPU:0, one launch (start us, length us, event | category | flops | bytes accessed | tf_op | source)
XLA Modules:
  0.0 680.8 jit_solution(1594376583155425065)
XLA Ops:
  7.4 2.1 constant_dynamic-slice_fusion.1
  11.8 3.0 collective-permute-start
  14.9 16.9 %collective-permute-done = bf16[112,2176]{1,0:T(8,128)(2,1)S(1)} collective-permute-done((bf16[112,2176]{1,0:T(8,128)(2,1)S(1)}, bf16[112,2176]{1,0:T(8,128)(2,1)S(1)}, u32[]{:S(2)}, u32[]{:S(2)}) %collective-permute-start) | collective-permute-done | bytes 487456 | tf_op jit(solution)/shard_map/ppermute | solution.py:156
  31.8 17.0 %collective-permute-done.1 = bf16[112,2176]{1,0:T(8,128)(2,1)S(1)} collective-permute-done((bf16[112,2176]{1,0:T(8,128)(2,1)S(1)}, bf16[112,2176]{1,0:T(8,128)(2,1)S(1)}, u32[]{:S(2)}, u32[]{:S(2)}) %collective-permute-start.1) | collective-permute-done | bytes 487456 | tf_op jit(solution)/shard_map/ppermute | solution.py:156
  48.8 23.9 %collective-permute-done.2 = bf16[112,2176]{1,0:T(8,128)(2,1)S(1)} collective-permute-done((bf16[112,2176]{1,0:T(8,128)(2,1)S(1)}, bf16[112,2176]{1,0:T(8,128)(2,1)S(1)}, u32[]{:S(2)}, u32[]{:S(2)}) %collective-permute-start.2) | collective-permute-done | bytes 487456 | tf_op jit(solution)/shard_map/ppermute | solution.py:156
  74.3 18.0 %collective-permute-done.3 = bf16[112,2176]{1,0:T(8,128)(2,1)S(1)} collective-permute-done((bf16[112,2176]{1,0:T(8,128)(2,1)S(1)}, bf16[112,2176]{1,0:T(8,128)(2,1)S(1)}, u32[]{:S(2)}, u32[]{:S(2)}) %collective-permute-start.3) | collective-permute-done | bytes 487456 | tf_op jit(solution)/shard_map/ppermute | solution.py:156
  93.2 17.1 %collective-permute-done.4 = bf16[112,2176]{1,0:T(8,128)(2,1)S(1)} collective-permute-done((bf16[112,2176]{1,0:T(8,128)(2,1)S(1)}, bf16[112,2176]{1,0:T(8,128)(2,1)S(1)}, u32[]{:S(2)}, u32[]{:S(2)}) %collective-permute-start.4) | collective-permute-done | bytes 487456 | tf_op jit(solution)/shard_map/ppermute | solution.py:156
  111.2 14.2 %collective-permute-done.5 = bf16[112,2176]{1,0:T(8,128)(2,1)S(1)} collective-permute-done((bf16[112,2176]{1,0:T(8,128)(2,1)S(1)}, bf16[112,2176]{1,0:T(8,128)(2,1)S(1)}, u32[]{:S(2)}, u32[]{:S(2)}) %collective-permute-start.5) | collective-permute-done | bytes 487456 | tf_op jit(solution)/shard_map/ppermute | solution.py:156
  125.9 9.6 %all_gather.40 = bf16[512,896]{1,0:T(8,128)(2,1)} all-gather(bf16[128,896]{1,0:T(8,128)(2,1)} %param.16), channel_id=1, replica_groups=mesh['rep'=4,'shard'=8] {'rep'}, dimensions={0}, use_global_device_ids=true | all-gather | bytes 1146880 | tf_op jit(solution)/shard_map/all_gather | solution.py:178
  135.5 12.3 %collective-permute-done.6 = bf16[112,2176]{1,0:T(8,128)(2,1)S(1)} collective-permute-done((bf16[112,2176]{1,0:T(8,128)(2,1)S(1)}, bf16[112,2176]{1,0:T(8,128)(2,1)S(1)}, u32[]{:S(2)}, u32[]{:S(2)}) %collective-permute-start.6) | collective-permute-done | bytes 487456 | tf_op jit(solution)/shard_map/ppermute | solution.py:156
  149.4 3.0 copy-done.3
  153.8 2.4 convolution_add_fusion
  157.5 2.4 multiply_reduce_fusion
  160.1 9.4 %all_gather.36 = bf16[512,896]{1,0:T(8,128)(2,1)} all-gather(bf16[128,896]{1,0:T(8,128)(2,1)S(1)} %multiply_convert_fusion.3), channel_id=1, replica_groups=mesh['rep'=4,'shard'=8] {'rep'}, dimensions={0}, use_global_device_ids=true | all-gather | bytes 1146880 | tf_op jit(solution)/shard_map/all_gather | solution.py:192
  169.5 4.9 fusion.69
  174.4 5.0 fusion.68
  179.4 31.2 %all-gather.14.cloned.1.call-done = bf16[1216,896]{1,0:T(8,128)(2,1)} async-done(((bf16[152,896]{1,0:T(8,128)(2,1)}), bf16[1216,896]{1,0:T(8,128)(2,1)}) %all-gather.14.cloned.1.call-update) | async-done | bytes 2179088 | tf_op jit(solution)/shard_map/all_gather | solution.py:175
  210.7 7.0 %multiply_convert_fusion = (bf16[512,1216]{0,1:T(8,128)(2,1)S(1)}, bf16[512,1216]{0,1:T(8,128)(2,1)S(1)}, bf16[512,1216]{0,1:T(8,128)(2,1)}) fusion(f32[512,1216]{0,1:T(8,128)} %fusion.68, f32[512,1216]{0,1:T(8,128)} %fusion.69, bf16[1216,896]{1,0:T(8,128)(2,1)} %all-gather.14.cloned.1.call-done, bf16[512,896]{1,0:T(8,128)(2,1)} %all_gather.40), kind=kOutput, calls=%fused_computation.7 | convolution fusion | flops 1125646336 | bytes 11812864 | tf_op jit(solution)/shard_map/dot_general | solution.py:16
  217.7 1.6 fusion.70
  220.2 2.6 add_convert_fusion
  222.9 4.5 convolution_convert_fusion.5
  227.4 4.5 convolution_convert_fusion.1
  232.0 4.4 convolution_convert_fusion.2
  236.7 4.5 convolution_convert_fusion
  241.3 4.2 reduce-scatter.12.cloned.1.call-done
  246.6 25.3 %reduce-scatter.10.cloned.1.call-done = bf16[128,896]{1,0:T(8,128)(2,1)} async-done(((bf16[512,896]{1,0:T(8,128)(2,1)}), bf16[128,896]{1,0:T(8,128)(2,1)}) %reduce-scatter.10.cloned.1.call-update) | async-done | bytes 229392 | tf_op jit(solution)/shard_map/reduce_scatter | solution.py:211
  271.9 1.9 fusion.24
  273.8 2.3 fusion.17
  277.8 2.5 fusion.37
  282.7 2.0 pad_maximum_fusion
  284.8 60.2 %reduce-scatter.20.cloned.1.call-done = bf16[112,1216]{1,0:T(8,128)(2,1)} async-done(((bf16[896,1216]{1,0:T(8,128)(2,1)}), bf16[112,1216]{1,0:T(8,128)(2,1)}) %reduce-scatter.20.cloned.1.call-update) | async-done | bytes 272400 | tf_op jit(solution)/shard_map/reduce_scatter | solution.py:209
  345.1 72.2 %reduce-scatter.18.cloned.1.call-done = bf16[112,1216]{1,0:T(8,128)(2,1)} async-done(((bf16[896,1216]{1,0:T(8,128)(2,1)}), bf16[112,1216]{1,0:T(8,128)(2,1)}) %reduce-scatter.18.cloned.1.call-update) | async-done | bytes 272400 | tf_op jit(solution)/shard_map/reduce_scatter | solution.py:208
  417.4 78.0 %reduce-scatter.22.cloned.1.call-done = bf16[152,896]{1,0:T(8,128)(2,1)} async-done(((bf16[1216,896]{1,0:T(8,128)(2,1)}), bf16[152,896]{1,0:T(8,128)(2,1)}) %reduce-scatter.22.cloned.1.call-update) | async-done | bytes 272400
  495.4 87.1 %reduce-scatter.14.cloned.1.call-done = bf16[112,2176]{1,0:T(8,128)(2,1)} async-done(((bf16[896,2176]{1,0:T(8,128)(2,1)}), bf16[112,2176]{1,0:T(8,128)(2,1)}) %reduce-scatter.14.cloned.1.call-update) | async-done | bytes 487440 | tf_op jit(solution)/shard_map/reduce_scatter | solution.py:247
  587.1 13.7 %all-gather.20.cloned.1.call-done = bf16[448,1216]{1,0:T(8,128)(2,1)} async-done(((bf16[112,1216]{1,0:T(8,128)(2,1)}), bf16[448,1216]{1,0:T(8,128)(2,1)}) %all-gather.20.cloned.1.call-update) | async-done | bytes 1089552 | tf_op jit(solution)/shard_map/all_gather | solution.py:263
  600.8 1.5 fusion.61
  602.2 1.9 fusion.60
  604.2 3.9 concatenate.114
  608.0 1.5 convert_element_type.175
  609.5 10.1 %all-gather.18.cloned.1.call-done = bf16[448,1216]{1,0:T(8,128)(2,1)} async-done(((bf16[112,1216]{1,0:T(8,128)(2,1)}), bf16[448,1216]{1,0:T(8,128)(2,1)}) %all-gather.18.cloned.1.call-update) | async-done | bytes 1089552 | tf_op jit(solution)/shard_map/all_gather | solution.py:263
  619.6 1.5 fusion.63
  621.1 1.9 fusion.62
  623.1 3.8 concatenate.113
  626.9 1.5 convert_element_type.173
  628.4 9.6 %all-gather.16.cloned.1.call-done = bf16[608,896]{1,0:T(8,128)(2,1)} async-done(((bf16[152,896]{1,0:T(8,128)(2,1)}), bf16[608,896]{1,0:T(8,128)(2,1)}) %all-gather.16.cloned.1.call-update) | async-done | bytes 1089552 | tf_op jit(solution)/shard_map/all_gather | solution.py:260
  638.0 2.7 convert_element_type.177
  640.7 21.7 %reduce-scatter.16.cloned.1.call-done = bf16[112,640]{1,0:T(8,128)(2,1)} async-done(((bf16[448,640]{1,0:T(8,128)(2,1)}), bf16[112,640]{1,0:T(8,128)(2,1)}) %reduce-scatter.16.cloned.1.call-update) | async-done | bytes 143376 | tf_op jit(solution)/shard_map/reduce_scatter | solution.py:254
  665.7 6.3 all-gather
  (189 shorter events, 27.1 us)
Async XLA Ops:
  7.2 65.5 %copy-start = (bf16[608,896]{1,0:T(8,128)(2,1)S(1)}, bf16[608,896]{1,0:T(8,128)(2,1)}, u32[]{:S(2)}) copy-start(bf16[608,896]{1,0:T(8,128)(2,1)} %param.28) | copy-start | bytes 3268612
  7.2 4.3 copy-start.17
  7.2 4.3 copy-start.18
  7.2 4.3 copy-start.16
  7.2 4.3 copy-start.15
  7.2 4.3 copy-start.14
  7.3 4.4 copy-start.4
  7.3 4.5 copy-start.8
  7.3 4.5 copy-start.9
  7.3 4.5 copy-start.5
  7.3 162.2 %all-gather.12.cloned.1.call-start = ((), (), s32[]{:S(2)}) async-start(), calls=%async_computation.8 | async-start | bytes 2580480 | tf_op jit(solution)/shard_map/all_gather | solution.py:174
  7.3 85.7 %copy-start.2 = (bf16[128,896]{1,0:T(8,128)(2,1)S(1)}, bf16[128,896]{1,0:T(8,128)(2,1)}, u32[]{:S(2)}) copy-start(bf16[128,896]{1,0:T(8,128)(2,1)} %param.15) | copy-start | bytes 688132
  10.4 164.1 %all-gather.10.cloned.1.call-start = ((), (), s32[]{:S(2)}) async-start(), calls=%async_computation.7 | async-start | bytes 2580480 | tf_op jit(solution)/shard_map/all_gather | solution.py:171
  11.4 199.2 %all-gather.14.cloned.1.call-start = ((), (), s32[]{:S(2)}) async-start(), calls=%async_computation.9 | async-start | bytes 2451456 | tf_op jit(solution)/shard_map/all_gather | solution.py:175
  11.8 19.9 %collective-permute-start = (bf16[112,2176]{1,0:T(8,128)(2,1)S(1)}, bf16[112,2176]{1,0:T(8,128)(2,1)S(1)}, u32[]{:S(2)}, u32[]{:S(2)}) collective-permute-start(bf16[112,2176]{1,0:T(8,128)(2,1)S(1)} %constant_dynamic-update-slice_fusion), channel_id=1, source_target_pairs={{0,1},{1,2},{2,3},{3,4},{4,5},{5,6},{6,7},{7,0},{8,9},{9,10},{10,1... | collective-permute-start | bytes 1462280 | tf_op jit(solution)/shard_map/ppermute | solution.py:156
  31.8 17.0 %collective-permute-start.1 = (bf16[112,2176]{1,0:T(8,128)(2,1)S(1)}, bf16[112,2176]{1,0:T(8,128)(2,1)S(1)}, u32[]{:S(2)}, u32[]{:S(2)}) collective-permute-start(bf16[112,2176]{1,0:T(8,128)(2,1)S(1)} %collective-permute-done), channel_id=1, source_target_pairs={{0,1},{1,2},{2,3},{3,4},{4,5},{5,6},{6,7},{7,0},{8,9},{9,10},{10,1... | collective-permute-start | bytes 1462280 | tf_op jit(solution)/shard_map/ppermute | solution.py:156
  48.8 23.9 %collective-permute-start.2 = (bf16[112,2176]{1,0:T(8,128)(2,1)S(1)}, bf16[112,2176]{1,0:T(8,128)(2,1)S(1)}, u32[]{:S(2)}, u32[]{:S(2)}) collective-permute-start(bf16[112,2176]{1,0:T(8,128)(2,1)S(1)} %collective-permute-done.1), channel_id=1, source_target_pairs={{0,1},{1,2},{2,3},{3,4},{4,5},{5,6},{6,7},{7,0},{8,9},{9,10},{10,1... | collective-permute-start | bytes 1462280 | tf_op jit(solution)/shard_map/ppermute | solution.py:156
  72.7 19.6 %collective-permute-start.3 = (bf16[112,2176]{1,0:T(8,128)(2,1)S(1)}, bf16[112,2176]{1,0:T(8,128)(2,1)S(1)}, u32[]{:S(2)}, u32[]{:S(2)}) collective-permute-start(bf16[112,2176]{1,0:T(8,128)(2,1)S(1)} %collective-permute-done.2), channel_id=1, source_target_pairs={{0,1},{1,2},{2,3},{3,4},{4,5},{5,6},{6,7},{7,0},{8,9},{9,10},{10,1... | collective-permute-start | bytes 1462280 | tf_op jit(solution)/shard_map/ppermute | solution.py:156
  73.4 172.1 %reduce-scatter.12.cloned.1.call-start = ((), (), s32[]{:S(2)}) async-start(), calls=%async_computation.11 | async-start | bytes 1146880 | tf_op jit(solution)/shard_map/reduce_scatter | solution.py:201
  92.3 18.0 %collective-permute-start.4 = (bf16[112,2176]{1,0:T(8,128)(2,1)S(1)}, bf16[112,2176]{1,0:T(8,128)(2,1)S(1)}, u32[]{:S(2)}, u32[]{:S(2)}) collective-permute-start(bf16[112,2176]{1,0:T(8,128)(2,1)S(1)} %collective-permute-done.3), channel_id=1, source_target_pairs={{0,1},{1,2},{2,3},{3,4},{4,5},{5,6},{6,7},{7,0},{8,9},{9,10},{10,1... | collective-permute-start | bytes 1462280 | tf_op jit(solution)/shard_map/ppermute | solution.py:156
  110.3 15.1 %collective-permute-start.5 = (bf16[112,2176]{1,0:T(8,128)(2,1)S(1)}, bf16[112,2176]{1,0:T(8,128)(2,1)S(1)}, u32[]{:S(2)}, u32[]{:S(2)}) collective-permute-start(bf16[112,2176]{1,0:T(8,128)(2,1)S(1)} %collective-permute-done.4), channel_id=1, source_target_pairs={{0,1},{1,2},{2,3},{3,4},{4,5},{5,6},{6,7},{7,0},{8,9},{9,10},{10,1... | collective-permute-start | bytes 1462280 | tf_op jit(solution)/shard_map/ppermute | solution.py:156
  125.4 22.4 %collective-permute-start.6 = (bf16[112,2176]{1,0:T(8,128)(2,1)S(1)}, bf16[112,2176]{1,0:T(8,128)(2,1)S(1)}, u32[]{:S(2)}, u32[]{:S(2)}) collective-permute-start(bf16[112,2176]{1,0:T(8,128)(2,1)S(1)} %collective-permute-done.5), channel_id=1, source_target_pairs={{0,1},{1,2},{2,3},{3,4},{4,5},{5,6},{6,7},{7,0},{8,9},{9,10},{10,1... | collective-permute-start | bytes 1462280 | tf_op jit(solution)/shard_map/ppermute | solution.py:156
  125.9 27.8 %copy-start.11 = (f32[128]{0:T(128)}, f32[128]{0:T(128)S(1)}, u32[]{:S(2)}) copy-start(f32[128]{0:T(128)S(1)} %get-tuple-element.137) | copy-start | bytes 1540
  147.9 0.9 copy-start.6
  149.4 3.1 copy-start.3
  153.8 3.0 copy-start.10
  210.7 7.0 %copy-start.20 = (bf16[896,1216]{1,0:T(8,128)(2,1)S(1)}, bf16[896,1216]{1,0:T(8,128)(2,1)}, u32[]{:S(2)}) copy-start(bf16[896,1216]{1,0:T(8,128)(2,1)} %all-gather.10.cloned.1.call-done) | copy-start | bytes 6537220
  217.7 1.6 copy-start.21
  217.7 1.6 copy-start.22
  217.7 2.5 copy-start.19
  222.8 49.1 %reduce-scatter.10.cloned.1.call-start = ((), (), s32[]{:S(2)}) async-start(), calls=%async_computation.10 | async-start | bytes 1146880 | tf_op jit(solution)/shard_map/reduce_scatter | solution.py:211
  227.4 117.7 %reduce-scatter.20.cloned.1.call-start = ((), (), s32[]{:S(2)}) async-start(), calls=%async_computation.15 | async-start | bytes 2580480 | tf_op jit(solution)/shard_map/reduce_scatter | solution.py:209
  231.9 185.3 %reduce-scatter.18.cloned.1.call-start = ((), (), s32[]{:S(2)}) async-start(), calls=%async_computation.14 | async-start | bytes 2580480 | tf_op jit(solution)/shard_map/reduce_scatter | solution.py:208
  236.4 258.9 %reduce-scatter.22.cloned.1.call-start = ((), (), s32[]{:S(2)}) async-start(), calls=%async_computation.19 | async-start | bytes 2451456
  241.2 30.7 %copy-start.7 = (bf16[128,896]{1,0:T(8,128)(2,1)S(1)}, bf16[128,896]{1,0:T(8,128)(2,1)}, u32[]{:S(2)}) copy-start(bf16[128,896]{1,0:T(8,128)(2,1)} %param.16) | copy-start | bytes 688132
  241.2 341.3 %reduce-scatter.14.cloned.1.call-start = ((), (), s32[]{:S(2)}) async-start(), calls=%async_computation.12 | async-start | bytes 4386816 | tf_op jit(solution)/shard_map/reduce_scatter | solution.py:247
  276.8 1.0 copy-start.12
  284.8 301.4 %copy-start.13 = (f32[128]{0:T(128)S(1)}, f32[128]{0:T(128)}, u32[]{:S(2)}) copy-start(f32[128]{0:T(128)} %get-tuple-element.136) | copy-start | bytes 1540
  284.8 316.0 %all-gather.20.cloned.1.call-start = ((), (), s32[]{:S(2)}) async-start(), calls=%async_computation.18 | async-start | bytes 1433600 | tf_op jit(solution)/shard_map/all_gather | solution.py:263
  345.1 274.5 %all-gather.18.cloned.1.call-start = ((), (), s32[]{:S(2)}) async-start(), calls=%async_computation.17 | async-start | bytes 1433600 | tf_op jit(solution)/shard_map/all_gather | solution.py:263
  417.3 220.7 %all-gather.16.cloned.1.call-start = ((), (), s32[]{:S(2)}) async-start(), calls=%async_computation.16 | async-start | bytes 1361920 | tf_op jit(solution)/shard_map/all_gather | solution.py:260
  495.4 167.1 %reduce-scatter.16.cloned.1.call-start = ((), (), s32[]{:S(2)}) async-start(), calls=%async_computation.13 | async-start | bytes 716800 | tf_op jit(solution)/shard_map/reduce_scatter | solution.py:254
  664.7 9.6 %copy-start.1 = (bf16[608,896]{1,0:T(8,128)(2,1)S(1)}, bf16[608,896]{1,0:T(8,128)(2,1)}, u32[]{:S(2)}) copy-start(bf16[608,896]{1,0:T(8,128)(2,1)} %param.28) | copy-start | bytes 3268612
Sparse Core Ops, SparseCore 0:
  10.9 73.7 all-gather.11
  87.4 70.4 all-gather.9
  160.7 49.8 all-gather.13
  223.0 22.4 reduce-scatter.11
  247.9 23.9 reduce-scatter.9
  275.3 69.7 reduce-scatter.19
  348.5 68.6 reduce-scatter.17
  421.3 74.0 reduce-scatter.21
  498.9 83.5 reduce-scatter.13
  583.9 16.7 all-gather.19
  602.3 17.2 all-gather.17
  621.0 16.9 all-gather.15
  640.5 21.9 reduce-scatter.15
